TPU v7x, 32 devices: a whole 2x2x4 slice. The times are simulated.
32 devices in a mesh: fsdp: 2 (over y), ctx: 4 (over z), tp: 4 (over x, core).
Axes of the slice: x: 2, y: 2, z: 4, core: 2. Of those that a mesh axis runs over, the one named last changes fastest.
Arguments:
- latent_in: bfloat16 [4, 1024, 768], P('fsdp', 'ctx'), may hold values from -6 to 6
- condition: bfloat16 [4, 768], P('fsdp'), may hold values from -6 to 6
- ada_weight: bfloat16 [768, 6, 768], P('fsdp', None, 'tp'), may hold values from -0.21875 to 0.21875
- ada_bias: float32 [6, 768], P(None, 'tp'), may hold values from -3 to 3
- qkv_weight: bfloat16 [768, 3, 768], P('fsdp', None, 'tp'), may hold values from -0.21875 to 0.21875
- qv_bias: float32 [2, 768], P(None, 'tp'), may hold values from -3 to 3
- out_weight: bfloat16 [768, 768], P('fsdp', 'tp'), may hold values from -2.5 to 2.5
- out_bias: float32 [768], replicated, may hold values from -3 to 3
- fc1_weight: bfloat16 [768, 3072], P('fsdp', 'tp'), may hold values from -0.21875 to 0.21875
- fc1_bias: float32 [3072], P('tp'), may hold values from -3 to 3
- fc2_weight: bfloat16 [768, 3072], P('fsdp', 'tp'), may hold values from -0.109375 to 0.109375
- fc2_bias: float32 [768], replicated, may hold values from -3 to 3
- out_grad: float32 [4, 1024, 768], P('fsdp', 'ctx'), may hold values from -6 to 6
Outputs:
- block_out: float32 [4, 1024, 768], P('fsdp', 'ctx')
- latent_grad: float32 [4, 1024, 768], P('fsdp', 'ctx')
- condition_grad: float32 [4, 768], P('fsdp')
- ada_weight_grad: float32 [768, 6, 768], P('fsdp', None, 'tp')
- ada_bias_grad: float32 [6, 768], P(None, 'tp')
- qkv_weight_grad: float32 [768, 3, 768], P('fsdp', None, 'tp')
- qv_bias_grad: float32 [2, 768], P(None, 'tp')
- out_weight_grad: float32 [768, 768], P('fsdp', 'tp')
- out_bias_grad: float32 [768], replicated
- fc1_weight_grad: float32 [768, 3072], P('fsdp', 'tp')
- fc1_bias_grad: float32 [3072], P('tp')
- fc2_weight_grad: float32 [768, 3072], P('fsdp', 'tp')
- fc2_bias_grad: float32 [768], replicated
All inputs are finite; a program needn't handle non-finite values.
Results may differ from a plain program's by a relative error of at most 0.009.
The roundings to bfloat16 on the way count: a program that leaves them out, or rounds other values in their place, can miss the bound.
Values may be sent and summed in bfloat16 or wider, within the bound.
A program may use at most 128 MiB of HBM per device.

v0:
```python
import jax
import jax.numpy as jnp
from jax import lax
from jax.sharding import PartitionSpec as P

HEAD_DIM = 64
EPS = 1e-06


def dot32(left, right):
    return jnp.dot(left, right, preferred_element_type=jnp.float32)


def rows_inner(left, right):
    return lax.dot_general(
        left, right, (((0,), (0,)), ((), ())), preferred_element_type=jnp.float32
    )


def last_inner(left, right):
    return lax.dot_general(
        left, right, (((left.ndim - 1,), (1,)), ((), ())), preferred_element_type=jnp.float32
    )


def norm_rows(values):
    centre = jnp.mean(values, axis=-1, keepdims=True)
    shifted = values - centre
    spread = jnp.mean(shifted * shifted, axis=-1, keepdims=True)
    inverse = lax.rsqrt(spread + EPS)
    return (shifted * inverse, inverse)


def norm_back(grad_norm, normed, inverse):
    first = jnp.mean(grad_norm, axis=-1, keepdims=True)
    second = jnp.mean(grad_norm * normed, axis=-1, keepdims=True)
    return inverse * (grad_norm - first - normed * second)


def gelu_fn(values):
    return jax.nn.gelu(values, approximate=True)


def local(
    latent_in,
    condition,
    ada_weight,
    ada_bias,
    qkv_weight,
    qv_bias,
    out_weight,
    out_bias,
    fc1_weight,
    fc1_bias,
    fc2_weight,
    fc2_bias,
    out_grad,
):
    full_ada, full_qkv, full_out, full_fc1, full_fc2 = (
        lax.all_gather(ada_weight, "fsdp", axis=0, tiled=True),
        lax.all_gather(qkv_weight, "fsdp", axis=0, tiled=True),
        lax.all_gather(out_weight, "fsdp", axis=0, tiled=True),
        lax.all_gather(fc1_weight, "fsdp", axis=0, tiled=True),
        lax.all_gather(fc2_weight, "fsdp", axis=0, tiled=True),
    )
    lat_count, seq_part, width_all = latent_in.shape
    head_cols = full_qkv.shape[2]
    heads_here = head_cols // HEAD_DIM
    row_count = lat_count * seq_part
    att_scale = HEAD_DIM ** (-0.5)
    cond_f = condition.astype(jnp.float32)
    cond_act = jax.nn.silu(cond_f).astype(jnp.bfloat16)
    mod_cols = (
        dot32(cond_act, full_ada.reshape(width_all, 6 * head_cols)).reshape(lat_count, 6, head_cols)
        + ada_bias
    )
    modulation = lax.all_gather(mod_cols, "tp", axis=2, tiled=True)
    shift_one = modulation[:, 0][:, None, :]
    scale_one = modulation[:, 1][:, None, :]
    gate_one = modulation[:, 2][:, None, :]
    shift_two = modulation[:, 3][:, None, :]
    scale_two = modulation[:, 4][:, None, :]
    gate_two = modulation[:, 5][:, None, :]
    latent_f = latent_in.astype(jnp.float32)
    norm_one, inv_one = norm_rows(latent_f)
    input_one = (norm_one * (1.0 + scale_one) + shift_one).astype(jnp.bfloat16)
    qkv_all = dot32(
        input_one.reshape(row_count, width_all), full_qkv.reshape(width_all, 3 * head_cols)
    ).reshape(lat_count, seq_part, 3, head_cols)
    queries = (qkv_all[:, :, 0] + qv_bias[0]).astype(jnp.bfloat16)
    keys_local = qkv_all[:, :, 1].astype(jnp.bfloat16)
    values_local = (qkv_all[:, :, 2] + qv_bias[1]).astype(jnp.bfloat16)
    keys_whole, values_whole = (
        lax.all_gather(keys_local, "ctx", axis=1, tiled=True),
        lax.all_gather(values_local, "ctx", axis=1, tiled=True),
    )
    seq_whole = keys_whole.shape[1]
    q_heads = queries.reshape(lat_count, seq_part, heads_here, HEAD_DIM)
    k_heads = keys_whole.reshape(lat_count, seq_whole, heads_here, HEAD_DIM)
    v_heads = values_whole.reshape(lat_count, seq_whole, heads_here, HEAD_DIM)
    scores = (
        jnp.einsum("bqhd,bkhd->bhqk", q_heads, k_heads, preferred_element_type=jnp.float32)
        * att_scale
    )
    row_max = jnp.max(scores, axis=-1, keepdims=True)
    log_total = row_max + jnp.log(jnp.sum(jnp.exp(scores - row_max), axis=-1, keepdims=True))
    probs_half = jnp.exp(scores - log_total).astype(jnp.bfloat16)
    mixed = jnp.einsum("bhqk,bkhd->bqhd", probs_half, v_heads, preferred_element_type=jnp.float32)
    mixed = mixed.reshape(lat_count, seq_part, head_cols).astype(jnp.bfloat16)
    attn_term = last_inner(mixed, full_out)
    attn_val = lax.psum(attn_term, "tp") + out_bias
    after_attn = latent_f + gate_one * attn_val
    norm_two, inv_two = norm_rows(after_attn)
    input_two = (norm_two * (1.0 + scale_two) + shift_two).astype(jnp.bfloat16)
    hidden_pre = dot32(input_two.reshape(row_count, width_all), full_fc1) + fc1_bias
    hidden_act = gelu_fn(hidden_pre).astype(jnp.bfloat16)
    mlp_term = last_inner(hidden_act, full_fc2).reshape(lat_count, seq_part, width_all)
    mlp_val = lax.psum(mlp_term.astype(jnp.bfloat16), "tp").astype(jnp.float32) + fc2_bias
    block_out = after_attn + gate_two * mlp_val
    grad_gate_two = jnp.sum(out_grad * mlp_val, axis=1)
    grad_mlp = out_grad * gate_two
    bias_fc2 = jnp.sum(grad_mlp, axis=(0, 1))
    grad_mlp_half = grad_mlp.astype(jnp.bfloat16).reshape(row_count, width_all)
    fc2_term = rows_inner(grad_mlp_half, hidden_act)
    grad_act = dot32(grad_mlp_half, full_fc2)
    grad_pre = jax.vjp(gelu_fn, hidden_pre)[1](grad_act)[0]
    bias_fc1 = jnp.sum(grad_pre, axis=0)
    grad_pre_half = grad_pre.astype(jnp.bfloat16)
    fc1_term = rows_inner(input_two.reshape(row_count, width_all), grad_pre_half)
    input_two_term = last_inner(grad_pre_half, full_fc1).reshape(lat_count, seq_part, width_all)
    grad_input_two = lax.psum(input_two_term, "tp")
    grad_shift_two = jnp.sum(grad_input_two, axis=1)
    grad_scale_two = jnp.sum(grad_input_two * norm_two, axis=1)
    grad_after = out_grad + norm_back(grad_input_two * (1.0 + scale_two), norm_two, inv_two)
    grad_gate_one = jnp.sum(grad_after * attn_val, axis=1)
    grad_attn = grad_after * gate_one
    bias_out = jnp.sum(grad_attn, axis=(0, 1))
    grad_attn_half = grad_attn.astype(jnp.bfloat16).reshape(row_count, width_all)
    out_term = rows_inner(grad_attn_half, mixed.reshape(row_count, head_cols))
    grad_mixed = (
        dot32(grad_attn_half, full_out)
        .astype(jnp.bfloat16)
        .reshape(lat_count, seq_part, heads_here, HEAD_DIM)
    )
    scores = (
        jnp.einsum("bqhd,bkhd->bhqk", q_heads, k_heads, preferred_element_type=jnp.float32)
        * att_scale
    )
    soft_probs = jnp.exp(scores - log_total)
    probs_half = soft_probs.astype(jnp.bfloat16)
    grad_v_whole = jnp.einsum(
        "bhqk,bqhd->bkhd", probs_half, grad_mixed, preferred_element_type=jnp.float32
    )
    grad_probs = jnp.einsum(
        "bqhd,bkhd->bhqk", grad_mixed, v_heads, preferred_element_type=jnp.float32
    )
    delta = jnp.sum(soft_probs * grad_probs, axis=-1, keepdims=True)
    grad_scores = (soft_probs * (grad_probs - delta) * att_scale).astype(jnp.bfloat16)
    grad_queries = jnp.einsum(
        "bhqk,bkhd->bqhd", grad_scores, k_heads, preferred_element_type=jnp.float32
    ).reshape(lat_count, seq_part, head_cols)
    grad_k_whole = jnp.einsum(
        "bhqk,bqhd->bkhd", grad_scores, q_heads, preferred_element_type=jnp.float32
    )
    grad_keys, grad_values = (
        lax.psum_scatter(
            grad_k_whole.reshape(lat_count, seq_whole, head_cols),
            "ctx",
            scatter_dimension=1,
            tiled=True,
        ),
        lax.psum_scatter(
            grad_v_whole.reshape(lat_count, seq_whole, head_cols),
            "ctx",
            scatter_dimension=1,
            tiled=True,
        ),
    )
    bias_qv = jnp.stack([jnp.sum(grad_queries, axis=(0, 1)), jnp.sum(grad_values, axis=(0, 1))])
    grad_qkv = (
        jnp.stack([grad_queries, grad_keys, grad_values], axis=2)
        .astype(jnp.bfloat16)
        .reshape(row_count, 3 * head_cols)
    )
    qkv_term = rows_inner(input_one.reshape(row_count, width_all), grad_qkv).reshape(
        width_all, 3, head_cols
    )
    input_one_term = last_inner(grad_qkv, full_qkv.reshape(width_all, 3 * head_cols)).reshape(
        lat_count, seq_part, width_all
    )
    grad_input_one = lax.psum(input_one_term, "tp")
    grad_shift_one = jnp.sum(grad_input_one, axis=1)
    grad_scale_one = jnp.sum(grad_input_one * norm_one, axis=1)
    latent_grad = grad_after + norm_back(grad_input_one * (1.0 + scale_one), norm_one, inv_one)
    grad_mod = jnp.stack(
        [
            grad_shift_one,
            grad_scale_one,
            grad_gate_one,
            grad_shift_two,
            grad_scale_two,
            grad_gate_two,
        ],
        axis=1,
    )
    mod_part = lax.dynamic_slice_in_dim(grad_mod, lax.axis_index("tp") * head_cols, head_cols, 2)
    bias_ada = jnp.sum(mod_part, axis=0)
    cond_term = jnp.einsum(
        "bje,dje->bd", mod_part, full_ada.astype(jnp.float32), precision=lax.Precision.HIGHEST
    )
    grad_cond_act = lax.psum(cond_term, ("ctx", "tp"))
    condition_grad = jax.vjp(jax.nn.silu, cond_f)[1](grad_cond_act)[0]
    bias_grads = lax.psum((bias_ada, bias_qv, bias_out, bias_fc1, bias_fc2), ("fsdp", "ctx"))
    ada_term = jnp.einsum(
        "bd,bje->dje", cond_act.astype(jnp.float32), mod_part, precision=lax.Precision.HIGHEST
    )
    weight_terms = (ada_term, qkv_term, out_term, fc1_term, fc2_term)
    pieces = (
        lax.psum_scatter(weight_terms[0], ("fsdp", "ctx"), scatter_dimension=0, tiled=True),
        lax.psum_scatter(weight_terms[1], ("fsdp", "ctx"), scatter_dimension=0, tiled=True),
        lax.psum_scatter(weight_terms[2], ("fsdp", "ctx"), scatter_dimension=0, tiled=True),
        lax.psum_scatter(weight_terms[3], ("fsdp", "ctx"), scatter_dimension=0, tiled=True),
        lax.psum_scatter(weight_terms[4], ("fsdp", "ctx"), scatter_dimension=0, tiled=True),
    )
    weight_grads = (
        lax.all_gather(pieces[0], "ctx", axis=0, tiled=True),
        lax.all_gather(pieces[1], "ctx", axis=0, tiled=True),
        lax.all_gather(pieces[2], "ctx", axis=0, tiled=True),
        lax.all_gather(pieces[3], "ctx", axis=0, tiled=True),
        lax.all_gather(pieces[4], "ctx", axis=0, tiled=True),
    )
    return (
        block_out,
        latent_grad,
        condition_grad,
        weight_grads[0],
        bias_grads[0],
        weight_grads[1],
        bias_grads[1],
        weight_grads[2],
        bias_grads[2],
        weight_grads[3],
        bias_grads[3],
        weight_grads[4],
        bias_grads[4],
    )


def solution(mesh):
    placed = (
        P("fsdp", "ctx", None),
        P("fsdp", None),
        P("fsdp", None, "tp"),
        P(None, "tp"),
        P("fsdp", None, "tp"),
        P(None, "tp"),
        P("fsdp", "tp"),
        P(),
        P("fsdp", "tp"),
        P("tp"),
        P("fsdp", "tp"),
        P(),
        P("fsdp", "ctx", None),
    )
    return jax.shard_map(
        local,
        mesh=mesh,
        in_specs=placed,
        out_specs=(
            P("fsdp", "ctx", None),
            P("fsdp", "ctx", None),
            P("fsdp", None),
            P("fsdp", None, "tp"),
            P(None, "tp"),
            P("fsdp", None, "tp"),
            P(None, "tp"),
            P("fsdp", "tp"),
            P(),
            P("fsdp", "tp"),
            P("tp"),
            P("fsdp", "tp"),
            P(),
        ),
        check_vma=False,
    )
```

profile of v0, /device:TPU:0, one launch (start us, length us, event | category | flops | bytes accessed | tf_op | source)
XLA Modules:
  0.0 946.5 jit_solution(13427247585707043213)
XLA Ops:
  10.0 7.9 all_gather.44
  18.4 21.4 %all_gather.41 = bf16[768,3,192]{0,2,1:T(8,128)(2,1)S(1)} all-gather(bf16[384,3,192]{0,2,1:T(8,128)(2,1)S(1)} %copy-done.25), channel_id=1, replica_groups=mesh['fsdp'=2,'ctx'=4,'tp'=4] {'fsdp'}, dimensions={0}, use_global_device_ids=true | all-gather | bytes 1327104 | tf_op jit(solution)/shard_map/all_gather | solution.py:61
  39.9 9.8 %all-gather.8.cloned.1.call-done = bf16[768,6,192]{0,2,1:T(8,128)(2,1)} async-done(((bf16[384,6,192]{0,2,1:T(8,128)(2,1)}), bf16[768,6,192]{0,2,1:T(8,128)(2,1)}) %all-gather.8.cloned.1.call-update) | async-done | bytes 1769488 | tf_op jit(solution)/shard_map/all_gather | solution.py:60
  49.7 2.0 fusion.41
  51.9 8.5 all_gather.40
  60.4 5.3 fusion.91
  65.7 1.9 copy.96
  71.1 19.8 %all-gather = bf16[2,1024,1,192]{1,3,2,0:T(8,128)(2,1)S(1)} all-gather(bf16[2,256,1,192]{1,3,2,0:T(8,128)(2,1)S(1)} %slice.61), channel_id=2, replica_groups=mesh['fsdp'=2,'ctx'=4,'tp'=4] {'ctx'}, dimensions={1}, use_global_device_ids=true | all-gather | bytes 983040 | tf_op jit(solution)/shard_map/all_gather | solution.py:94
  91.0 18.0 %all_gather.42 = bf16[2,1024,192]{1,2,0:T(8,128)(2,1)S(1)} all-gather(bf16[2,256,192]{1,2,0:T(8,128)(2,1)S(1)} %fusion.52), channel_id=1, replica_groups=mesh['fsdp'=2,'ctx'=4,'tp'=4] {'ctx'}, dimensions={1}, use_global_device_ids=true | all-gather | bytes 983040 | tf_op jit(solution)/shard_map/all_gather | solution.py:95
  117.1 1.9 copy.81
  120.3 37.4 %all-reduce.6.cloned.1.call-done = f32[2,256,768]{2,1,0:T(8,128)} async-done(((f32[2,256,768]{2,1,0:T(8,128)}), f32[2,256,768]{2,1,0:T(8,128)}) %all-reduce.6.cloned.1.call-update) | async-done | bytes 1572880 | tf_op jit(solution)/shard_map/psum | solution.py:111
  157.7 1.7 fusion.90
  161.3 20.8 %all-gather.10.cloned.1.call-done = bf16[768,768]{1,0:T(8,128)(2,1)} async-done(((bf16[384,768]{1,0:T(8,128)(2,1)}), bf16[768,768]{1,0:T(8,128)(2,1)}) %all-gather.10.cloned.1.call-update) | async-done | bytes 1179664 | tf_op jit(solution)/shard_map/all_gather | solution.py:63
  182.1 3.4 convolution_add_fusion
  185.5 20.7 %all-gather.12.cloned.1.call-done = bf16[768,768]{1,0:T(8,128)(2,1)} async-done(((bf16[384,768]{1,0:T(8,128)(2,1)}), bf16[768,768]{1,0:T(8,128)(2,1)}) %all-gather.12.cloned.1.call-update) | async-done | bytes 1179664 | tf_op jit(solution)/shard_map/all_gather | solution.py:64
  206.3 3.7 convolution_convert_fusion
  211.5 33.6 %all-reduce.8.cloned.1.call-done = bf16[2,256,768]{2,1,0:T(8,128)(2,1)} async-done(((bf16[2,256,768]{2,1,0:T(8,128)(2,1)}), bf16[2,256,768]{2,1,0:T(8,128)(2,1)}) %all-reduce.8.cloned.1.call-update) | async-done | bytes 786448 | tf_op jit(solution)/shard_map/psum | solution.py:118
  245.2 2.7 multiply_reduce_fusion.8
  247.9 2.2 fusion.88
  250.1 2.0 fusion.55
  252.1 43.0 %all-reduce.10.cloned.1.call-done = f32[2,256,768]{2,1,0:T(8,128)} async-done(((f32[2,256,768]{2,1,0:T(8,128)}), f32[2,256,768]{2,1,0:T(8,128)}) %all-reduce.10.cloned.1.call-update) | async-done | bytes 1572880 | tf_op jit(solution)/shard_map/psum | solution.py:131
  295.1 2.9 multiply_reduce_fusion.3
  298.0 4.5 multiply_reduce_fusion.7
  304.3 5.2 fusion.48
  310.6 3.7 fusion.60
  314.2 18.8 %fusion.6 = f32[2,3,64,1024]{3,2,1,0:T(8,128)} fusion(f32[2,3,256,1024]{3,2,1,0:T(8,128)} %fusion.60, f32[2,3,256,1024]{3,2,1,0:T(8,128)} %copy-done, f32[2,3,256]{2,1,0:T(4,128)S(1)} %copy-done.29, f32[2,256,3,64]{1,3,2,0:T(8,128)} %bitcast.144, f32[3,64]{1,0:T(4,128)S(1)} %copy-done.42), kind=kOutput, calls=%fused_computation.8 | convolution fusion | flops 215681536 | bytes 14555904 | tf_op jit(solution)/shard_map/bhqk,bqhd->bkhd/dot_general | solution.py:162
  334.2 16.0 %bitcast_reduce_fusion = (f32[3,64]{1,0:T(4,128)S(1)}, bf16[2,3,64,256]{3,2,1,0:T(8,128)(2,1)S(1)}) fusion(bf16[2,1024,3,64]{1,3,2,0:T(8,128)(2,1)S(1)} %bitcast.138, f32[2,3,256,1024]{3,2,1,0:T(8,128)} %fusion.60, f32[2,3,256,1024]{3,2,1,0:T(8,128)} %copy-done, f32[2,3,256]{2,1,0:T(4,128)S(1)} %copy-done.29), kind=kOutput, calls=%fused_computation.76 | convolution fusion | flops 215681344 | bytes 13572864 | tf_op jit(solution)/shard_map/bhqk,bkhd->bqhd/dot_general | solution.py:159
  350.3 31.5 %reduce-scatter.8.cloned.1.call-done = f32[2,256,192]{1,2,0:T(8,128)} async-done(((f32[2,1024,192]{1,2,0:T(8,128)}), f32[2,256,192]{1,2,0:T(8,128)}) %reduce-scatter.8.cloned.1.call-update) | async-done | bytes 393232 | tf_op jit(solution)/shard_map/reduce_scatter | solution.py:166
  383.8 2.0 convolution_bitcast_fusion
  386.9 3.4 fusion.53
  391.4 3.8 fusion.87
  395.4 32.3 %all-reduce.12.cloned.1.call-done = f32[2,256,768]{2,1,0:T(8,128)} async-done(((f32[2,256,768]{2,1,0:T(8,128)}), f32[2,256,768]{2,1,0:T(8,128)}) %all-reduce.12.cloned.1.call-update) | async-done | bytes 1572880 | tf_op jit(solution)/shard_map/psum | solution.py:191
  427.7 2.2 fusion.33
  430.0 4.2 fusion.69
  436.4 64.2 %reduce-scatter.18.cloned.1.call-done = f32[96,768]{1,0:T(8,128)} async-done(((f32[768,768]{1,0:T(8,128)}), f32[96,768]{1,0:T(8,128)}) %reduce-scatter.18.cloned.1.call-update) | async-done | bytes 294928 | tf_op jit(solution)/shard_map/reduce_scatter | solution.py:222
  500.7 72.5 %reduce-scatter.20.cloned.1.call-done = f32[96,768]{1,0:T(8,128)} async-done(((f32[768,768]{1,0:T(8,128)}), f32[96,768]{1,0:T(8,128)}) %reduce-scatter.20.cloned.1.call-update) | async-done | bytes 294928 | tf_op jit(solution)/shard_map/reduce_scatter | solution.py:223
  574.0 2.3 fusion.94
  576.3 95.2 %reduce-scatter.12.cloned.1.call-done = f32[96,6,192]{2,0,1:T(8,128)} async-done(((f32[768,6,192]{2,0,1:T(8,128)}), f32[96,6,192]{2,0,1:T(8,128)}) %reduce-scatter.12.cloned.1.call-update) | async-done | bytes 442384 | tf_op jit(solution)/shard_map/reduce_scatter | solution.py:219
  671.6 66.7 %reduce-scatter.16.cloned.1.call-done = f32[96,192]{1,0:T(8,128)} async-done(((f32[768,192]{1,0:T(8,128)}), f32[96,192]{1,0:T(8,128)}) %reduce-scatter.16.cloned.1.call-update) | async-done | bytes 73744 | tf_op jit(solution)/shard_map/reduce_scatter | solution.py:221
  738.3 16.5 %all_gather.49 = f32[384,192]{1,0:T(8,128)S(1)} all-gather(f32[96,192]{1,0:T(8,128)} %reduce-scatter.16.cloned.1.call-done), channel_id=1, replica_groups=mesh['fsdp'=2,'ctx'=4,'tp'=4] {'ctx'}, dimensions={0}, use_global_device_ids=true | all-gather | bytes 368640 | tf_op jit(solution)/shard_map/all_gather | solution.py:228
  756.0 37.8 %all-reduce = (f32[6,192]{1,0:T(8,128)}, f32[2,192]{1,0:T(2,128)}, f32[768]{0:T(1024)}, f32[768]{0:T(1024)}, f32[768]{0:T(1024)}) all-reduce(f32[6,192]{1,0:T(8,128)S(1)} %dynamic-slice_reduce_fusion, f32[2,192]{1,0:T(2,128)S(1)} %pad_maximum_fusion, ...), channel_id=1, replica_groups=mesh['fsdp'=2,'ctx'=4,'tp'=4] {'fsdp','ctx'}, use_global_device_ids=true, to_apply=%region_26.27 | all-reduce | flops 3840 | bytes 30720 | tf_op jit(solution)/shard_map/psum | solution.py:213
  793.8 2.4 convolution_bitcast_fusion.2
  796.2 30.8 %psum.74 = f32[2,768]{1,0:T(2,128)S(1)} all-reduce(f32[2,768]{1,0:T(2,128)S(1)} %convolution_bitcast_fusion.2), channel_id=1, replica_groups=mesh['fsdp'=2,'ctx'=4,'tp'=4] {'ctx','tp'}, use_global_device_ids=true, to_apply=%region_23.24 | all-reduce | flops 1536 | bytes 12288 | tf_op jit(solution)/shard_map/psum | solution.py:211
  827.6 3.1 fusion.32
  830.7 43.6 %reduce-scatter.14.cloned.1.call-done = f32[96,3,192]{2,0,1:T(8,128)} async-done(((f32[768,3,192]{2,0,1:T(8,128)}), f32[96,3,192]{2,0,1:T(8,128)}) %reduce-scatter.14.cloned.1.call-update) | async-done | bytes 221200 | tf_op jit(solution)/shard_map/reduce_scatter | solution.py:220
  874.3 33.9 %all_gather.48 = f32[384,3,192]{2,0,1:T(8,128)S(1)} all-gather(f32[96,3,192]{2,0,1:T(8,128)} %reduce-scatter.14.cloned.1.call-done), channel_id=1, replica_groups=mesh['fsdp'=2,'ctx'=4,'tp'=4] {'ctx'}, dimensions={0}, use_global_device_ids=true | all-gather | bytes 1105920 | tf_op jit(solution)/shard_map/all_gather | solution.py:227
  909.5 24.9 %all-gather.14.cloned.1.call-done = f32[384,6,192]{2,0,1:T(8,128)} async-done(((f32[96,6,192]{2,0,1:T(8,128)}), f32[384,6,192]{2,0,1:T(8,128)}) %all-gather.14.cloned.1.call-update) | async-done | bytes 1769488 | tf_op jit(solution)/shard_map/all_gather | solution.py:226
  934.3 2.9 copy.88
  (197 shorter events, 37.3 us)
Async XLA Ops:
  7.2 10.7 %copy-start.1 = (bf16[2,256,768]{2,1,0:T(8,128)(2,1)S(1)}, bf16[2,256,768]{2,1,0:T(8,128)(2,1)}, u32[]{:S(2)}) copy-start(bf16[2,256,768]{2,1,0:T(8,128)(2,1)} %param.13) | copy-start | bytes 2359300
  7.2 11.2 %copy-start.25 = (bf16[384,3,192]{0,2,1:T(8,128)(2,1)S(1)}, bf16[384,3,192]{0,2,1:T(8,128)(2,1)}, u32[]{:S(2)}) copy-start(bf16[384,3,192]{0,2,1:T(8,128)(2,1)} %param.17) | copy-start | bytes 1327108
  7.2 42.5 %all-gather.8.cloned.1.call-start = ((), (), s32[]{:S(2)}) async-start(), calls=%async_computation.7 | async-start | bytes 2654208 | tf_op jit(solution)/shard_map/all_gather | solution.py:60
  7.9 149.7 %all-reduce.6.cloned.1.call-start = ((), (), s32[]{:S(2)}) async-start(), calls=%async_computation.8 | async-start | bytes 3145728 | tf_op jit(solution)/shard_map/psum | solution.py:111
  10.0 39.7 %copy-start.34 = (bf16[2,768]{1,0:T(2,128)(2,1)S(1)}, bf16[2,768]{1,0:T(2,128)(2,1)}, u32[]{:S(2)}) copy-start(bf16[2,768]{1,0:T(2,128)(2,1)} %param.14) | copy-start | bytes 9220
  10.0 39.7 %copy-start.47 = (f32[6,192]{1,0:T(8,128)S(1)}, f32[6,192]{1,0:T(8,128)}, u32[]{:S(2)}) copy-start(f32[6,192]{1,0:T(8,128)} %param.16) | copy-start | bytes 13828
  18.1 51.1 %copy-start.30 = (f32[2,256]{1,0:T(2,128)}, f32[2,256]{1,0:T(2,128)S(1)}, u32[]{:S(2)}) copy-start(f32[2,256]{1,0:T(2,128)S(1)} %broadcast_multiply_fusion.5) | copy-start | bytes 6148
  39.9 30.4 %copy-start.9 = (bf16[768,3,192]{0,2,1:T(8,128)(2,1)}, bf16[768,3,192]{0,2,1:T(8,128)(2,1)S(1)}, u32[]{:S(2)}) copy-start(bf16[768,3,192]{0,2,1:T(8,128)(2,1)S(1)} %all_gather.41) | copy-start | bytes 2654212
  39.9 29.3 %copy-start.32 = (f32[2,256]{1,0:T(2,128)}, f32[2,256]{1,0:T(2,128)S(1)}, u32[]{:S(2)}) copy-start(f32[2,256]{1,0:T(2,128)S(1)} %add_rsqrt_fusion.1) | copy-start | bytes 6148
  70.9 38.0 %copy-start.41 = (f32[3,64]{1,0:T(4,128)S(1)}, f32[3,64]{1,0:T(4,128)}, u32[]{:S(2)}) copy-start(f32[3,64]{1,0:T(4,128)} %add.180) | copy-start | bytes 2308
  71.0 39.2 %copy-start.18 = (f32[2,256,1,192]{1,3,2,0:T(8,128)}, f32[2,256,1,192]{1,3,2,0:T(8,128)S(1)}, u32[]{:S(2)}) copy-start(f32[2,256,1,192]{1,3,2,0:T(8,128)S(1)} %slice.49) | copy-start | bytes 1179652
  91.0 19.2 %copy-start.12 = (bf16[2,1024,1,192]{1,3,2,0:T(8,128)(2,1)}, bf16[2,1024,1,192]{1,3,2,0:T(8,128)(2,1)S(1)}, u32[]{:S(2)}) copy-start(bf16[2,1024,1,192]{1,3,2,0:T(8,128)(2,1)S(1)} %all-gather) | copy-start | bytes 2359300
  115.7 3.3 copy-start.11
  115.7 66.4 %all-gather.10.cloned.1.call-start = ((), (), s32[]{:S(2)}) async-start(), calls=%async_computation.9 | async-start | bytes 1769472 | tf_op jit(solution)/shard_map/all_gather | solution.py:63
  116.5 89.8 %all-gather.12.cloned.1.call-start = ((), (), s32[]{:S(2)}) async-start(), calls=%async_computation.10 | async-start | bytes 1769472 | tf_op jit(solution)/shard_map/all_gather | solution.py:64
  117.0 128.1 %all-reduce.8.cloned.1.call-start = ((), (), s32[]{:S(2)}) async-start(), calls=%async_computation.11 | async-start | bytes 1572864 | tf_op jit(solution)/shard_map/psum | solution.py:118
  159.8 22.3 %copy-start.52 = (f32[768]{0:T(1024)S(1)}, f32[768]{0:T(1024)}, u32[]{:S(2)}) copy-start(f32[768]{0:T(1024)} %param.22) | copy-start | bytes 9220
  210.0 35.2 %copy-start.44 = (f32[768]{0:T(1024)S(1)}, f32[768]{0:T(1024)}, u32[]{:S(2)}) copy-start(f32[768]{0:T(1024)} %param.24) | copy-start | bytes 9220
  210.0 85.1 %all-reduce.10.cloned.1.call-start = ((), (), s32[]{:S(2)}) async-start(), calls=%async_computation.12 | async-start | bytes 3145728 | tf_op jit(solution)/shard_map/psum | solution.py:131
  252.1 45.9 %copy-start.43 = (f32[768]{0:T(1024)S(1)}, f32[768]{0:T(1024)}, u32[]{:S(2)}) copy-start(f32[768]{0:T(1024)} %param.20) | copy-start | bytes 9220
  252.1 98.2 %reduce-scatter.10.cloned.1.call-start = ((), (), s32[]{:S(2)}) async-start(), calls=%async_computation.14 | async-start | bytes 1966080 | tf_op jit(solution)/shard_map/reduce_scatter | solution.py:172
  309.5 4.8 copy-start.29
  309.5 4.8 copy-start.42
  309.5 72.3 %reduce-scatter.8.cloned.1.call-start = ((), (), s32[]{:S(2)}) async-start(), calls=%async_computation.13 | async-start | bytes 1966080 | tf_op jit(solution)/shard_map/reduce_scatter | solution.py:166
  333.1 94.6 %all-reduce.12.cloned.1.call-start = ((), (), s32[]{:S(2)}) async-start(), calls=%async_computation.15 | async-start | bytes 3145728 | tf_op jit(solution)/shard_map/psum | solution.py:191
  350.2 33.6 %copy-start.10 = (bf16[768,3,192]{0,2,1:T(8,128)(2,1)S(1)}, bf16[768,3,192]{0,2,1:T(8,128)(2,1)}, u32[]{:S(2)}) copy-start(bf16[768,3,192]{0,2,1:T(8,128)(2,1)} %copy-done.9) | copy-start | bytes 2654212
  385.8 114.8 %reduce-scatter.18.cloned.1.call-start = ((), (), s32[]{:S(2)}) async-start(), calls=%async_computation.20 | async-start | bytes 2654208 | tf_op jit(solution)/shard_map/reduce_scatter | solution.py:222
  390.3 182.9 %reduce-scatter.20.cloned.1.call-start = ((), (), s32[]{:S(2)}) async-start(), calls=%async_computation.22 | async-start | bytes 2654208 | tf_op jit(solution)/shard_map/reduce_scatter | solution.py:223
  395.2 32.4 %copy-start.31 = (f32[2,256]{1,0:T(2,128)S(1)}, f32[2,256]{1,0:T(2,128)}, u32[]{:S(2)}) copy-start(f32[2,256]{1,0:T(2,128)} %copy-done.30) | copy-start | bytes 6148
  395.2 32.4 %copy-start.33 = (f32[2,256]{1,0:T(2,128)S(1)}, f32[2,256]{1,0:T(2,128)}, u32[]{:S(2)}) copy-start(f32[2,256]{1,0:T(2,128)} %copy-done.32) | copy-start | bytes 6148
  395.3 34.6 %copy-start.38 = (f32[2,768]{1,0:T(2,128)S(1)}, f32[2,768]{1,0:T(2,128)}, u32[]{:S(2)}) copy-start(f32[2,768]{1,0:T(2,128)} %get-tuple-element.87) | copy-start | bytes 18436
  395.3 34.6 %copy-start.40 = (f32[2,768]{1,0:T(2,128)S(1)}, f32[2,768]{1,0:T(2,128)}, u32[]{:S(2)}) copy-start(f32[2,768]{1,0:T(2,128)} %get-tuple-element.88) | copy-start | bytes 18436
  395.3 34.6 %copy-start.39 = (f32[2,768]{1,0:T(2,128)S(1)}, f32[2,768]{1,0:T(2,128)}, u32[]{:S(2)}) copy-start(f32[2,768]{1,0:T(2,128)} %get-tuple-element.78) | copy-start | bytes 18436
  395.3 34.6 %copy-start.37 = (f32[2,768]{1,0:T(2,128)S(1)}, f32[2,768]{1,0:T(2,128)}, u32[]{:S(2)}) copy-start(f32[2,768]{1,0:T(2,128)} %get-tuple-element.85) | copy-start | bytes 18436
  395.3 34.6 %copy-start.35 = (bf16[2,768]{1,0:T(2,128)(2,1)S(1)}, bf16[2,768]{1,0:T(2,128)(2,1)}, u32[]{:S(2)}) copy-start(bf16[2,768]{1,0:T(2,128)(2,1)} %param.14) | copy-start | bytes 9220
  395.3 276.2 %reduce-scatter.12.cloned.1.call-start = ((), (), s32[]{:S(2)}) async-start(), calls=%async_computation.16 | async-start | bytes 5308416 | tf_op jit(solution)/shard_map/reduce_scatter | solution.py:219
  434.2 139.1 %copy-start.15 = (bf16[2,256,3,192]{1,3,2,0:T(8,128)(2,1)S(1)}, bf16[2,256,3,192]{1,3,2,0:T(8,128)(2,1)}, u32[]{:S(2)}) copy-start(bf16[2,256,3,192]{1,3,2,0:T(8,128)(2,1)} %copy-done.14) | copy-start | bytes 1769476
  434.2 304.1 %reduce-scatter.16.cloned.1.call-start = ((), (), s32[]{:S(2)}) async-start(), calls=%async_computation.19 | async-start | bytes 884736 | tf_op jit(solution)/shard_map/reduce_scatter | solution.py:221
  436.4 394.3 %all-gather.16.cloned.1.call-start = ((), (), s32[]{:S(2)}) async-start(), calls=%async_computation.21 | async-start | bytes 1474560 | tf_op jit(solution)/shard_map/all_gather | solution.py:229
  500.7 330.1 %all-gather.18.cloned.1.call-start = ((), (), s32[]{:S(2)}) async-start(), calls=%async_computation.23 | async-start | bytes 1474560 | tf_op jit(solution)/shard_map/all_gather | solution.py:230
  573.2 301.2 %reduce-scatter.14.cloned.1.call-start = ((), (), s32[]{:S(2)}) async-start(), calls=%async_computation.18 | async-start | bytes 2654208 | tf_op jit(solution)/shard_map/reduce_scatter | solution.py:220
  576.2 179.5 %copy-start.19 = (f32[2,256,192]{1,2,0:T(8,128)S(1)}, f32[2,256,192]{1,2,0:T(8,128)}, u32[]{:S(2)}) copy-start(f32[2,256,192]{1,2,0:T(8,128)} %reduce-scatter.10.cloned.1.call-done) | copy-start | bytes 1179652
  576.3 179.7 %copy-start.45 = (f32[768]{0:T(1024)S(1)}, f32[768]{0:T(1024)}, u32[]{:S(2)}) copy-start(f32[768]{0:T(1024)} %get-tuple-element.84) | copy-start | bytes 9220
  576.3 179.7 %copy-start.46 = (f32[768]{0:T(1024)S(1)}, f32[768]{0:T(1024)}, u32[]{:S(2)}) copy-start(f32[768]{0:T(1024)} %get-tuple-element.86) | copy-start | bytes 9220
  576.3 179.7 %copy-start.49 = (f32[768]{0:T(1024)S(1)}, f32[768]{0:T(1024)}, u32[]{:S(2)}) copy-start(f32[768]{0:T(1024)} %get-tuple-element.95) | copy-start | bytes 9220
  576.3 358.0 %all-gather.14.cloned.1.call-start = ((), (), s32[]{:S(2)}) async-start(), calls=%async_computation.17 | async-start | bytes 2949120 | tf_op jit(solution)/shard_map/all_gather | solution.py:226
  754.8 72.8 %copy-start.3 = (f32[2,256,768]{2,1,0:T(8,128)S(1)}, f32[2,256,768]{2,1,0:T(8,128)}, u32[]{:S(2)}) copy-start(f32[2,256,768]{2,1,0:T(8,128)} %copy-done.2) | copy-start | bytes 4718596
  909.5 27.8 %copy-start.20 = (f32[384,768]{1,0:T(8,128)S(1)}, f32[384,768]{1,0:T(8,128)}, u32[]{:S(2)}) copy-start(f32[384,768]{1,0:T(8,128)} %all-gather.16.cloned.1.call-done) | copy-start | bytes 3538948
  (23 other events, 38.8 us)
Sparse Core Ops, SparseCore 0:
  9.5 40.0 all-gather.7
  115.8 41.8 all-reduce.5
  159.2 22.8 all-gather.9
  183.5 22.7 all-gather.11
  210.1 35.0 all-reduce.7
  252.2 42.8 all-reduce.9
  309.6 35.5 reduce-scatter.9
  347.5 34.2 reduce-scatter.7
  385.9 41.6 all-reduce.11
  431.0 69.5 reduce-scatter.17
  504.1 68.9 reduce-scatter.19
  576.7 94.8 reduce-scatter.11
  675.4 62.8 reduce-scatter.15
  739.7 30.9 all-gather.15
  772.1 29.7 all-gather.17
  805.2 69.0 reduce-scatter.13
  875.8 58.5 all-gather.13
where the time goes:
time: 948 us; the launch traced here: 946 us
  waiting for transfers between devices  598 us (63%)
  blocking collectives  195 us (21%)
  matrix products  81.3 us (9%)
  local copies, waits for them, and re-layouts  31.6 us (3%)
  other arithmetic  25.1 us (3%)
  between operations  14.6 us (2%)
    reduce_scatter x1, waiting for transfers between devices, local(): lax.psum_scatter(weight_terms[0], ('fsdp', 'ctx'), scatter_dimension=0, t...  95.2 us
    reduce_scatter x1, waiting for transfers between devices, local(): lax.psum_scatter(weight_terms[4], ('fsdp', 'ctx'), scatter_dimension=0, t...  72.5 us
    reduce_scatter x1, waiting for transfers between devices, local(): lax.psum_scatter(weight_terms[2], ('fsdp', 'ctx'), scatter_dimension=0, t...  66.7 us
    reduce_scatter x1, waiting for transfers between devices, local(): lax.psum_scatter(weight_terms[3], ('fsdp', 'ctx'), scatter_dimension=0, t...  64.2 us
    reduce_scatter x1, waiting for transfers between devices, local(): lax.psum_scatter(weight_terms[1], ('fsdp', 'ctx'), scatter_dimension=0, t...  43.6 us
    psum x1, waiting for transfers between devices, local(): grad_input_two = lax.psum(input_two_term, 'tp')  43 us
    psum x1, blocking collectives, local(): lax.psum((bias_ada, bias_qv, bias_out, bias_fc1, bias_fc2), ('fsdp', 'ctx'))  37.8 us
    psum x1, waiting for transfers between devices, local(): attn_val = lax.psum(attn_term, 'tp') + out_bias  37.4 us
  transfers between devices with their start and end apart: 17, of which 14 were waited for; matrix products, arithmetic and copies ran while one was open for 8% of the time, Pallas kernels for 0%

commit v1 on v0

--- a/solution.py
+++ b/solution.py
@@ -108,7 +108,7 @@
     mixed = jnp.einsum("bhqk,bkhd->bqhd", probs_half, v_heads, preferred_element_type=jnp.float32)
     mixed = mixed.reshape(lat_count, seq_part, head_cols).astype(jnp.bfloat16)
     attn_term = last_inner(mixed, full_out)
-    attn_val = lax.psum(attn_term, "tp") + out_bias
+    attn_val = jnp.sum(lax.all_gather(attn_term, "tp"), axis=0) + out_bias
     after_attn = latent_f + gate_one * attn_val
     norm_two, inv_two = norm_rows(after_attn)
     input_two = (norm_two * (1.0 + scale_two) + shift_two).astype(jnp.bfloat16)

time: 948 us -> 958 us (1.011)
    all_gather x0 -> x1, waiting for transfers between devices: none -> 40.4 us  [local(): attn_val = jnp.sum(lax.all_gather(attn_term, 'tp'), axis=0) + out_bias]
    psum x1 -> x0, waiting for transfers between devices: 37.4 us -> none  [local(): attn_val = lax.psum(attn_term, 'tp') + out_bias]
  transfers between devices with their start and end apart: 17 -> 17, of which waited for: 14 -> 14; matrix products, arithmetic and copies ran while one was open for 8% -> 9% of each run, Pallas kernels for 0% -> 0%
where the time goes in v1:
time: 958 us; the launch traced here: 951 us
  waiting for transfers between devices  597 us (62%)
  blocking collectives  195 us (20%)
  matrix products  81.3 us (8%)
  local copies, waits for them, and re-layouts  32.8 us (3%)
  other arithmetic  28.9 us (3%)
  between operations  14.8 us (2%)
    reduce_scatter x1, waiting for transfers between devices, local(): lax.psum_scatter(weight_terms[0], ('fsdp', 'ctx'), scatter_dimension=0, t...  95.2 us
    reduce_scatter x1, waiting for transfers between devices, local(): lax.psum_scatter(weight_terms[4], ('fsdp', 'ctx'), scatter_dimension=0, t...  72.4 us
    reduce_scatter x1, waiting for transfers between devices, local(): lax.psum_scatter(weight_terms[2], ('fsdp', 'ctx'), scatter_dimension=0, t...  66.7 us
    reduce_scatter x1, waiting for transfers between devices, local(): lax.psum_scatter(weight_terms[3], ('fsdp', 'ctx'), scatter_dimension=0, t...  64.2 us
    reduce_scatter x1, waiting for transfers between devices, local(): lax.psum_scatter(weight_terms[1], ('fsdp', 'ctx'), scatter_dimension=0, t...  43.8 us
    psum x1, waiting for transfers between devices, local(): grad_input_two = lax.psum(input_two_term, 'tp')  43 us
    all_gather x1, waiting for transfers between devices, local(): attn_val = jnp.sum(lax.all_gather(attn_term, 'tp'), axis=0) + out_bias  40.4 us
    psum x1, blocking collectives, local(): lax.psum((bias_ada, bias_qv, bias_out, bias_fc1, bias_fc2), ('fsdp', 'ctx'))  37.8 us
  transfers between devices with their start and end apart: 17, of which 14 were waited for; matrix products, arithmetic and copies ran while one was open for 9% of the time, Pallas kernels for 0%

profile of v1, /device:TPU:0, one launch (start us, length us, event | category | flops | bytes accessed | tf_op | source)
XLA Modules:
  0.0 950.7 jit_solution(15278481020390757086)
XLA Ops:
  10.0 7.9 all_gather.50
  18.4 21.4 %all_gather.47 = bf16[768,3,192]{0,2,1:T(8,128)(2,1)S(1)} all-gather(bf16[384,3,192]{0,2,1:T(8,128)(2,1)S(1)} %copy-done.25), channel_id=1, replica_groups=mesh['fsdp'=2,'ctx'=4,'tp'=4] {'fsdp'}, dimensions={0}, use_global_device_ids=true | all-gather | bytes 1327104 | tf_op jit(solution)/shard_map/all_gather | solution.py:61
  39.9 9.8 %all-gather.10.cloned.1.call-done = bf16[768,6,192]{0,2,1:T(8,128)(2,1)} async-done(((bf16[384,6,192]{0,2,1:T(8,128)(2,1)}), bf16[768,6,192]{0,2,1:T(8,128)(2,1)}) %all-gather.10.cloned.1.call-update) | async-done | bytes 1769488 | tf_op jit(solution)/shard_map/all_gather | solution.py:60
  49.7 2.0 fusion.41
  51.9 8.5 all_gather.46
  60.4 5.4 fusion.91
  67.0 1.9 copy.78
  70.9 19.8 %all-gather = bf16[2,1024,1,192]{1,3,2,0:T(8,128)(2,1)S(1)} all-gather(bf16[2,256,1,192]{1,3,2,0:T(8,128)(2,1)S(1)} %slice.61), channel_id=2, replica_groups=mesh['fsdp'=2,'ctx'=4,'tp'=4] {'ctx'}, dimensions={1}, use_global_device_ids=true | all-gather | bytes 983040 | tf_op jit(solution)/shard_map/all_gather | solution.py:94
  90.7 18.0 %all_gather.48 = bf16[2,1024,192]{1,2,0:T(8,128)(2,1)S(1)} all-gather(bf16[2,256,192]{1,2,0:T(8,128)(2,1)S(1)} %fusion.52), channel_id=1, replica_groups=mesh['fsdp'=2,'ctx'=4,'tp'=4] {'ctx'}, dimensions={1}, use_global_device_ids=true | all-gather | bytes 983040 | tf_op jit(solution)/shard_map/all_gather | solution.py:95
  118.0 1.9 copy.81
  121.2 40.4 %all-gather.22.cloned.1.call-done = f32[8,256,768]{2,1,0:T(8,128)} async-done(((f32[2,256,768]{2,1,0:T(8,128)}), f32[8,256,768]{2,1,0:T(8,128)}) %all-gather.22.cloned.1.call-update) | async-done | bytes 6291472 | tf_op jit(solution)/shard_map/all_gather | solution.py:111
  161.6 4.5 reduce_sum.210
  169.8 16.2 %all-gather.12.cloned.1.call-done = bf16[768,768]{1,0:T(8,128)(2,1)} async-done(((bf16[384,768]{1,0:T(8,128)(2,1)}), bf16[768,768]{1,0:T(8,128)(2,1)}) %all-gather.12.cloned.1.call-update) | async-done | bytes 1179664 | tf_op jit(solution)/shard_map/all_gather | solution.py:63
  186.0 3.4 convolution_add_fusion
  189.4 20.7 %all-gather.14.cloned.1.call-done = bf16[768,768]{1,0:T(8,128)(2,1)} async-done(((bf16[384,768]{1,0:T(8,128)(2,1)}), bf16[768,768]{1,0:T(8,128)(2,1)}) %all-gather.14.cloned.1.call-update) | async-done | bytes 1179664 | tf_op jit(solution)/shard_map/all_gather | solution.py:64
  210.1 3.7 convolution_convert_fusion
  215.2 33.8 %all-reduce.5.cloned.1.call-done = bf16[2,256,768]{2,1,0:T(8,128)(2,1)} async-done(((bf16[2,256,768]{2,1,0:T(8,128)(2,1)}), bf16[2,256,768]{2,1,0:T(8,128)(2,1)}) %all-reduce.5.cloned.1.call-update) | async-done | bytes 786448 | tf_op jit(solution)/shard_map/psum | solution.py:118
  249.0 2.7 multiply_reduce_fusion.8
  251.7 2.2 fusion.88
  253.9 2.0 fusion.55
  256.0 43.0 %all-reduce.7.cloned.1.call-done = f32[2,256,768]{2,1,0:T(8,128)} async-done(((f32[2,256,768]{2,1,0:T(8,128)}), f32[2,256,768]{2,1,0:T(8,128)}) %all-reduce.7.cloned.1.call-update) | async-done | bytes 1572880 | tf_op jit(solution)/shard_map/psum | solution.py:131
  298.9 2.9 multiply_reduce_fusion.3
  301.8 4.5 multiply_reduce_fusion.7
  308.1 5.2 fusion.48
  314.4 3.7 fusion.60
  318.1 18.8 %fusion.6 = f32[2,3,64,1024]{3,2,1,0:T(8,128)} fusion(f32[2,3,256,1024]{3,2,1,0:T(8,128)} %fusion.60, f32[2,3,256,1024]{3,2,1,0:T(8,128)} %copy-done, f32[2,3,256]{2,1,0:T(4,128)S(1)} %copy-done.29, f32[2,256,3,64]{1,3,2,0:T(8,128)} %bitcast.146, f32[3,64]{1,0:T(4,128)S(1)} %copy-done.42), kind=kOutput, calls=%fused_computation.8 | convolution fusion | flops 215681536 | bytes 14555904 | tf_op jit(solution)/shard_map/bhqk,bqhd->bkhd/dot_general | solution.py:162
  338.0 16.0 %bitcast_reduce_fusion = (f32[3,64]{1,0:T(4,128)S(1)}, bf16[2,3,64,256]{3,2,1,0:T(8,128)(2,1)S(1)}) fusion(bf16[2,1024,3,64]{1,3,2,0:T(8,128)(2,1)S(1)} %bitcast.140, f32[2,3,256,1024]{3,2,1,0:T(8,128)} %fusion.60, f32[2,3,256,1024]{3,2,1,0:T(8,128)} %copy-done, f32[2,3,256]{2,1,0:T(4,128)S(1)} %copy-done.29), kind=kOutput, calls=%fused_computation.76 | convolution fusion | flops 215681344 | bytes 13572864 | tf_op jit(solution)/shard_map/bhqk,bkhd->bqhd/dot_general | solution.py:159
  354.1 31.5 %reduce-scatter.8.cloned.1.call-done = f32[2,256,192]{1,2,0:T(8,128)} async-done(((f32[2,1024,192]{1,2,0:T(8,128)}), f32[2,256,192]{1,2,0:T(8,128)}) %reduce-scatter.8.cloned.1.call-update) | async-done | bytes 393232 | tf_op jit(solution)/shard_map/reduce_scatter | solution.py:166
  387.6 2.0 convolution_bitcast_fusion
  390.7 3.4 fusion.53
  395.3 3.8 fusion.87
  399.4 32.1 %all-reduce.9.cloned.1.call-done = f32[2,256,768]{2,1,0:T(8,128)} async-done(((f32[2,256,768]{2,1,0:T(8,128)}), f32[2,256,768]{2,1,0:T(8,128)}) %all-reduce.9.cloned.1.call-update) | async-done | bytes 1572880 | tf_op jit(solution)/shard_map/psum | solution.py:191
  431.5 2.2 fusion.33
  433.8 4.2 fusion.69
  440.3 64.2 %reduce-scatter.18.cloned.1.call-done = f32[96,768]{1,0:T(8,128)} async-done(((f32[768,768]{1,0:T(8,128)}), f32[96,768]{1,0:T(8,128)}) %reduce-scatter.18.cloned.1.call-update) | async-done | bytes 294928 | tf_op jit(solution)/shard_map/reduce_scatter | solution.py:222
  504.5 72.4 %reduce-scatter.20.cloned.1.call-done = f32[96,768]{1,0:T(8,128)} async-done(((f32[768,768]{1,0:T(8,128)}), f32[96,768]{1,0:T(8,128)}) %reduce-scatter.20.cloned.1.call-update) | async-done | bytes 294928 | tf_op jit(solution)/shard_map/reduce_scatter | solution.py:223
  577.7 2.3 fusion.94
  580.1 95.2 %reduce-scatter.12.cloned.1.call-done = f32[96,6,192]{2,0,1:T(8,128)} async-done(((f32[768,6,192]{2,0,1:T(8,128)}), f32[96,6,192]{2,0,1:T(8,128)}) %reduce-scatter.12.cloned.1.call-update) | async-done | bytes 442384 | tf_op jit(solution)/shard_map/reduce_scatter | solution.py:219
  675.4 66.7 %reduce-scatter.16.cloned.1.call-done = f32[96,192]{1,0:T(8,128)} async-done(((f32[768,192]{1,0:T(8,128)}), f32[96,192]{1,0:T(8,128)}) %reduce-scatter.16.cloned.1.call-update) | async-done | bytes 73744 | tf_op jit(solution)/shard_map/reduce_scatter | solution.py:221
  742.1 16.5 %all_gather.57 = f32[384,192]{1,0:T(8,128)S(1)} all-gather(f32[96,192]{1,0:T(8,128)} %reduce-scatter.16.cloned.1.call-done), channel_id=1, replica_groups=mesh['fsdp'=2,'ctx'=4,'tp'=4] {'ctx'}, dimensions={0}, use_global_device_ids=true | all-gather | bytes 368640 | tf_op jit(solution)/shard_map/all_gather | solution.py:228
  759.7 37.8 %all-reduce = (f32[6,192]{1,0:T(8,128)}, f32[2,192]{1,0:T(2,128)}, f32[768]{0:T(1024)}, f32[768]{0:T(1024)}, f32[768]{0:T(1024)}) all-reduce(f32[6,192]{1,0:T(8,128)S(1)} %dynamic-slice_reduce_fusion, f32[2,192]{1,0:T(2,128)S(1)} %pad_maximum_fusion, ...), channel_id=1, replica_groups=mesh['fsdp'=2,'ctx'=4,'tp'=4] {'fsdp','ctx'}, use_global_device_ids=true, to_apply=%region_26.27 | all-reduce | flops 3840 | bytes 30720 | tf_op jit(solution)/shard_map/psum | solution.py:213
  797.5 2.4 convolution_bitcast_fusion.2
  800.0 30.8 %psum.66 = f32[2,768]{1,0:T(2,128)S(1)} all-reduce(f32[2,768]{1,0:T(2,128)S(1)} %convolution_bitcast_fusion.2), channel_id=1, replica_groups=mesh['fsdp'=2,'ctx'=4,'tp'=4] {'ctx','tp'}, use_global_device_ids=true, to_apply=%region_23.24 | all-reduce | flops 1536 | bytes 12288 | tf_op jit(solution)/shard_map/psum | solution.py:211
  831.4 3.1 fusion.32
  834.5 43.8 %reduce-scatter.14.cloned.1.call-done = f32[96,3,192]{2,0,1:T(8,128)} async-done(((f32[768,3,192]{2,0,1:T(8,128)}), f32[96,3,192]{2,0,1:T(8,128)}) %reduce-scatter.14.cloned.1.call-update) | async-done | bytes 221200 | tf_op jit(solution)/shard_map/reduce_scatter | solution.py:220
  878.3 33.9 %all_gather.56 = f32[384,3,192]{2,0,1:T(8,128)S(1)} all-gather(f32[96,3,192]{2,0,1:T(8,128)} %reduce-scatter.14.cloned.1.call-done), channel_id=1, replica_groups=mesh['fsdp'=2,'ctx'=4,'tp'=4] {'ctx'}, dimensions={0}, use_global_device_ids=true | all-gather | bytes 1105920 | tf_op jit(solution)/shard_map/all_gather | solution.py:227
  913.4 24.9 %all-gather.16.cloned.1.call-done = f32[384,6,192]{2,0,1:T(8,128)} async-done(((f32[96,6,192]{2,0,1:T(8,128)}), f32[384,6,192]{2,0,1:T(8,128)}) %all-gather.16.cloned.1.call-update) | async-done | bytes 1769488 | tf_op jit(solution)/shard_map/all_gather | solution.py:226
  938.3 2.9 copy.88
  (198 shorter events, 39.8 us)
Async XLA Ops:
  7.2 10.7 %copy-start.1 = (bf16[2,256,768]{2,1,0:T(8,128)(2,1)S(1)}, bf16[2,256,768]{2,1,0:T(8,128)(2,1)}, u32[]{:S(2)}) copy-start(bf16[2,256,768]{2,1,0:T(8,128)(2,1)} %param.13) | copy-start | bytes 2359300
  7.2 11.2 %copy-start.25 = (bf16[384,3,192]{0,2,1:T(8,128)(2,1)S(1)}, bf16[384,3,192]{0,2,1:T(8,128)(2,1)}, u32[]{:S(2)}) copy-start(bf16[384,3,192]{0,2,1:T(8,128)(2,1)} %param.17) | copy-start | bytes 1327108
  7.2 42.5 %all-gather.10.cloned.1.call-start = ((), (), s32[]{:S(2)}) async-start(), calls=%async_computation.7 | async-start | bytes 2654208 | tf_op jit(solution)/shard_map/all_gather | solution.py:60
  7.9 153.7 %all-gather.22.cloned.1.call-start = ((), (), s32[]{:S(2)}) async-start(), calls=%async_computation.23 | async-start | bytes 7864320 | tf_op jit(solution)/shard_map/all_gather | solution.py:111
  10.0 39.7 %copy-start.34 = (bf16[2,768]{1,0:T(2,128)(2,1)S(1)}, bf16[2,768]{1,0:T(2,128)(2,1)}, u32[]{:S(2)}) copy-start(bf16[2,768]{1,0:T(2,128)(2,1)} %param.14) | copy-start | bytes 9220
  10.0 39.7 %copy-start.47 = (f32[6,192]{1,0:T(8,128)S(1)}, f32[6,192]{1,0:T(8,128)}, u32[]{:S(2)}) copy-start(f32[6,192]{1,0:T(8,128)} %param.16) | copy-start | bytes 13828
  18.1 50.9 %copy-start.30 = (f32[2,256]{1,0:T(2,128)}, f32[2,256]{1,0:T(2,128)S(1)}, u32[]{:S(2)}) copy-start(f32[2,256]{1,0:T(2,128)S(1)} %broadcast_multiply_fusion.5) | copy-start | bytes 6148
  39.9 30.1 %copy-start.9 = (bf16[768,3,192]{0,2,1:T(8,128)(2,1)}, bf16[768,3,192]{0,2,1:T(8,128)(2,1)S(1)}, u32[]{:S(2)}) copy-start(bf16[768,3,192]{0,2,1:T(8,128)(2,1)S(1)} %all_gather.47) | copy-start | bytes 2654212
  39.9 29.1 %copy-start.32 = (f32[2,256]{1,0:T(2,128)}, f32[2,256]{1,0:T(2,128)S(1)}, u32[]{:S(2)}) copy-start(f32[2,256]{1,0:T(2,128)S(1)} %add_rsqrt_fusion.1) | copy-start | bytes 6148
  70.7 38.0 %copy-start.41 = (f32[3,64]{1,0:T(4,128)S(1)}, f32[3,64]{1,0:T(4,128)}, u32[]{:S(2)}) copy-start(f32[3,64]{1,0:T(4,128)} %add.178) | copy-start | bytes 2308
  70.8 39.1 %copy-start.18 = (f32[2,256,1,192]{1,3,2,0:T(8,128)}, f32[2,256,1,192]{1,3,2,0:T(8,128)S(1)}, u32[]{:S(2)}) copy-start(f32[2,256,1,192]{1,3,2,0:T(8,128)S(1)} %slice.49) | copy-start | bytes 1179652
  90.7 19.2 %copy-start.12 = (bf16[2,1024,1,192]{1,3,2,0:T(8,128)(2,1)}, bf16[2,1024,1,192]{1,3,2,0:T(8,128)(2,1)S(1)}, u32[]{:S(2)}) copy-start(bf16[2,1024,1,192]{1,3,2,0:T(8,128)(2,1)S(1)} %all-gather) | copy-start | bytes 2359300
  116.1 3.7 copy-start.11
  116.1 69.8 %all-gather.12.cloned.1.call-start = ((), (), s32[]{:S(2)}) async-start(), calls=%async_computation.8 | async-start | bytes 1769472 | tf_op jit(solution)/shard_map/all_gather | solution.py:63
  116.9 93.3 %all-gather.14.cloned.1.call-start = ((), (), s32[]{:S(2)}) async-start(), calls=%async_computation.9 | async-start | bytes 1769472 | tf_op jit(solution)/shard_map/all_gather | solution.py:64
  117.5 131.6 %all-reduce.5.cloned.1.call-start = ((), (), s32[]{:S(2)}) async-start(), calls=%async_computation.10 | async-start | bytes 1572864 | tf_op jit(solution)/shard_map/psum | solution.py:118
  161.6 4.5 copy-start.43
  168.2 17.8 %copy-start.52 = (f32[768]{0:T(1024)S(1)}, f32[768]{0:T(1024)}, u32[]{:S(2)}) copy-start(f32[768]{0:T(1024)} %param.22) | copy-start | bytes 9220
  213.8 35.2 %copy-start.44 = (f32[768]{0:T(1024)S(1)}, f32[768]{0:T(1024)}, u32[]{:S(2)}) copy-start(f32[768]{0:T(1024)} %param.24) | copy-start | bytes 9220
  213.9 85.0 %all-reduce.7.cloned.1.call-start = ((), (), s32[]{:S(2)}) async-start(), calls=%async_computation.11 | async-start | bytes 3145728 | tf_op jit(solution)/shard_map/psum | solution.py:131
  255.9 98.2 %reduce-scatter.10.cloned.1.call-start = ((), (), s32[]{:S(2)}) async-start(), calls=%async_computation.13 | async-start | bytes 1966080 | tf_op jit(solution)/shard_map/reduce_scatter | solution.py:172
  313.3 4.8 copy-start.29
  313.3 4.8 copy-start.42
  313.3 72.3 %reduce-scatter.8.cloned.1.call-start = ((), (), s32[]{:S(2)}) async-start(), calls=%async_computation.12 | async-start | bytes 1966080 | tf_op jit(solution)/shard_map/reduce_scatter | solution.py:166
  336.9 94.6 %all-reduce.9.cloned.1.call-start = ((), (), s32[]{:S(2)}) async-start(), calls=%async_computation.14 | async-start | bytes 3145728 | tf_op jit(solution)/shard_map/psum | solution.py:191
  354.1 33.6 %copy-start.10 = (bf16[768,3,192]{0,2,1:T(8,128)(2,1)S(1)}, bf16[768,3,192]{0,2,1:T(8,128)(2,1)}, u32[]{:S(2)}) copy-start(bf16[768,3,192]{0,2,1:T(8,128)(2,1)} %copy-done.9) | copy-start | bytes 2654212
  389.6 114.8 %reduce-scatter.18.cloned.1.call-start = ((), (), s32[]{:S(2)}) async-start(), calls=%async_computation.19 | async-start | bytes 2654208 | tf_op jit(solution)/shard_map/reduce_scatter | solution.py:222
  394.1 182.8 %reduce-scatter.20.cloned.1.call-start = ((), (), s32[]{:S(2)}) async-start(), calls=%async_computation.21 | async-start | bytes 2654208 | tf_op jit(solution)/shard_map/reduce_scatter | solution.py:223
  399.1 32.4 %copy-start.31 = (f32[2,256]{1,0:T(2,128)S(1)}, f32[2,256]{1,0:T(2,128)}, u32[]{:S(2)}) copy-start(f32[2,256]{1,0:T(2,128)} %copy-done.30) | copy-start | bytes 6148
  399.1 32.4 %copy-start.33 = (f32[2,256]{1,0:T(2,128)S(1)}, f32[2,256]{1,0:T(2,128)}, u32[]{:S(2)}) copy-start(f32[2,256]{1,0:T(2,128)} %copy-done.32) | copy-start | bytes 6148
  399.1 34.6 %copy-start.38 = (f32[2,768]{1,0:T(2,128)S(1)}, f32[2,768]{1,0:T(2,128)}, u32[]{:S(2)}) copy-start(f32[2,768]{1,0:T(2,128)} %get-tuple-element.87) | copy-start | bytes 18436
  399.1 34.6 %copy-start.40 = (f32[2,768]{1,0:T(2,128)S(1)}, f32[2,768]{1,0:T(2,128)}, u32[]{:S(2)}) copy-start(f32[2,768]{1,0:T(2,128)} %get-tuple-element.88) | copy-start | bytes 18436
  399.1 34.6 %copy-start.39 = (f32[2,768]{1,0:T(2,128)S(1)}, f32[2,768]{1,0:T(2,128)}, u32[]{:S(2)}) copy-start(f32[2,768]{1,0:T(2,128)} %get-tuple-element.78) | copy-start | bytes 18436
  399.1 34.6 %copy-start.37 = (f32[2,768]{1,0:T(2,128)S(1)}, f32[2,768]{1,0:T(2,128)}, u32[]{:S(2)}) copy-start(f32[2,768]{1,0:T(2,128)} %get-tuple-element.85) | copy-start | bytes 18436
  399.1 34.6 %copy-start.35 = (bf16[2,768]{1,0:T(2,128)(2,1)S(1)}, bf16[2,768]{1,0:T(2,128)(2,1)}, u32[]{:S(2)}) copy-start(bf16[2,768]{1,0:T(2,128)(2,1)} %param.14) | copy-start | bytes 9220
  399.2 276.1 %reduce-scatter.12.cloned.1.call-start = ((), (), s32[]{:S(2)}) async-start(), calls=%async_computation.15 | async-start | bytes 5308416 | tf_op jit(solution)/shard_map/reduce_scatter | solution.py:219
  438.0 139.0 %copy-start.15 = (bf16[2,256,3,192]{1,3,2,0:T(8,128)(2,1)S(1)}, bf16[2,256,3,192]{1,3,2,0:T(8,128)(2,1)}, u32[]{:S(2)}) copy-start(bf16[2,256,3,192]{1,3,2,0:T(8,128)(2,1)} %copy-done.14) | copy-start | bytes 1769476
  438.0 304.1 %reduce-scatter.16.cloned.1.call-start = ((), (), s32[]{:S(2)}) async-start(), calls=%async_computation.18 | async-start | bytes 884736 | tf_op jit(solution)/shard_map/reduce_scatter | solution.py:221
  440.2 394.3 %all-gather.18.cloned.1.call-start = ((), (), s32[]{:S(2)}) async-start(), calls=%async_computation.20 | async-start | bytes 1474560 | tf_op jit(solution)/shard_map/all_gather | solution.py:229
  504.5 330.0 %all-gather.20.cloned.1.call-start = ((), (), s32[]{:S(2)}) async-start(), calls=%async_computation.22 | async-start | bytes 1474560 | tf_op jit(solution)/shard_map/all_gather | solution.py:230
  576.9 301.3 %reduce-scatter.14.cloned.1.call-start = ((), (), s32[]{:S(2)}) async-start(), calls=%async_computation.17 | async-start | bytes 2654208 | tf_op jit(solution)/shard_map/reduce_scatter | solution.py:220
  580.0 179.5 %copy-start.19 = (f32[2,256,192]{1,2,0:T(8,128)S(1)}, f32[2,256,192]{1,2,0:T(8,128)}, u32[]{:S(2)}) copy-start(f32[2,256,192]{1,2,0:T(8,128)} %reduce-scatter.10.cloned.1.call-done) | copy-start | bytes 1179652
  580.0 179.7 %copy-start.45 = (f32[768]{0:T(1024)S(1)}, f32[768]{0:T(1024)}, u32[]{:S(2)}) copy-start(f32[768]{0:T(1024)} %get-tuple-element.84) | copy-start | bytes 9220
  580.0 179.7 %copy-start.46 = (f32[768]{0:T(1024)S(1)}, f32[768]{0:T(1024)}, u32[]{:S(2)}) copy-start(f32[768]{0:T(1024)} %get-tuple-element.86) | copy-start | bytes 9220
  580.0 179.7 %copy-start.49 = (f32[768]{0:T(1024)S(1)}, f32[768]{0:T(1024)}, u32[]{:S(2)}) copy-start(f32[768]{0:T(1024)} %get-tuple-element.95) | copy-start | bytes 9220
  580.0 358.3 %all-gather.16.cloned.1.call-start = ((), (), s32[]{:S(2)}) async-start(), calls=%async_computation.16 | async-start | bytes 2949120 | tf_op jit(solution)/shard_map/all_gather | solution.py:226
  758.6 72.8 %copy-start.3 = (f32[2,256,768]{2,1,0:T(8,128)S(1)}, f32[2,256,768]{2,1,0:T(8,128)}, u32[]{:S(2)}) copy-start(f32[2,256,768]{2,1,0:T(8,128)} %copy-done.2) | copy-start | bytes 4718596
  913.4 27.8 %copy-start.20 = (f32[384,768]{1,0:T(8,128)S(1)}, f32[384,768]{1,0:T(8,128)}, u32[]{:S(2)}) copy-start(f32[384,768]{1,0:T(8,128)} %all-gather.18.cloned.1.call-done) | copy-start | bytes 3538948
  (23 other events, 38.0 us)
Sparse Core Ops, SparseCore 0:
  9.5 40.0 all-gather.9
  116.3 45.3 all-gather.21
  163.2 22.7 all-gather.11
  187.4 22.7 all-gather.13
  214.0 34.9 all-reduce.4
  256.0 42.8 all-reduce.6
  313.4 35.5 reduce-scatter.9
  351.3 34.2 reduce-scatter.7
  389.7 41.6 all-reduce.8
  434.8 69.6 reduce-scatter.17
  508.0 68.8 reduce-scatter.19
  580.4 94.8 reduce-scatter.11
  679.2 62.8 reduce-scatter.15
  743.5 30.9 all-gather.17
  775.9 29.7 all-gather.19
  809.0 69.1 reduce-scatter.13
  879.7 58.5 all-gather.15
